TPU v7x, 256 devices: a whole 4x4x8 slice. The times are simulated.
256 devices in a mesh: dp: 4 (over y_hi, core), expert: 64 (over x, z, y_lo).
Axes of the slice: x: 4, y: 4 (y_hi: 2, y_lo: 2; y = y_hi * 2 + y_lo), z: 8, core: 2. Of those that a mesh axis runs over, the one named last changes fastest.
Arguments:
- tokens: bfloat16 [4, 8192, 3584], P('dp', 'expert'), may hold values from -6 to 6
- cotangent: bfloat16 [4, 8192, 1024], P('dp', 'expert'), may hold values from -12 to 12
- gate_weights: float32 [4, 8192], replicated, may hold values from 0.1 to 1
- tile_expert: int32 [4, 64], replicated, may hold values from 0 to 63, as said below
- w_gate: bfloat16 [64, 3584, 1024], P('expert', None, 'dp'), may hold values from -0.09375 to 0.09375
- w_up: bfloat16 [64, 3584, 1024], P('expert', None, 'dp'), may hold values from -0.09375 to 0.09375
Outputs:
- d_tokens: bfloat16 [4, 8192, 3584], P('dp', 'expert')
- hidden: bfloat16 [4, 8192, 1024], P(None, 'expert', 'dp')
- grad_gate: bfloat16 [64, 3584, 1024], P('expert', None, 'dp')
- grad_up: bfloat16 [64, 3584, 1024], P('expert', None, 'dp')
Inputs may be any that keep to these rules, and one draw needn't show every extreme that they name: tile_expert[g, j] is either j or (j + 1) mod 64: the expert of the tile's own index of the expert axis or of the next index round the closed cycle.
All inputs are finite; a program needn't handle non-finite values.
Results may differ from a plain program's by a relative error of at most 0.009.
Values may be sent and summed in bfloat16 or wider, within the bound.
A program may use at most 128 MiB of HBM per device.

v0:
```python
import jax
import jax.numpy as jnp
from jax import lax
from jax.sharding import Mesh
from jax.sharding import PartitionSpec as P

TILE = 128
DP = ("dp_0", "dp_1")


def in_blocks(x, dim, count):
    before, after = (x.shape[:dim], x.shape[dim + 1 :])
    return jnp.moveaxis(x.reshape(*before, count, -1, *after), dim, 0)


def joined_along(pieces, dim):
    dims = list(pieces.shape[1:])
    dims[dim] *= pieces.shape[0]
    return jnp.moveaxis(pieces, 0, dim).reshape(dims)


def exchange_in_order(pieces, axes, order):
    inside = pieces.shape[1:]
    out = pieces.reshape(*(lax.axis_size(a) for a in axes), *inside)
    for k in order:
        out = lax.all_to_all(out, axes[k], k, k, tiled=True)
    return out.reshape(-1, *inside)


def core_and_chips(x, groups, order, split_dim, concat_dim):
    count = lax.axis_size(groups[0]) * lax.axis_size(groups[1])
    pieces = in_blocks(x, split_dim, count)
    return joined_along(exchange_in_order(pieces, groups, order), concat_dim)


def shifted(value, axis, steps):
    count = lax.axis_size(axis)
    pairs = [(source, (source + steps) % count) for source in range(count)]
    return lax.ppermute(value, axis, pairs)


def sent_and_summed(x, axis, dim):
    count = lax.axis_size(axis)
    pieces = lax.all_to_all(in_blocks(x, dim, count), axis, 0, 0, tiled=True)
    return jnp.sum(pieces.astype(jnp.float32), axis=0)


def contract(left, right, left_axis, right_axis):
    return lax.dot_general(
        left, right, (((left_axis,), (right_axis,)), ((), ())), preferred_element_type=jnp.float32
    )


def route_scale(tile_expert, gate_weights, source, expert, row_count):
    tile_count = row_count // TILE
    owners = lax.dynamic_slice_in_dim(tile_expert, source * tile_count, tile_count, 1)
    weights = lax.dynamic_slice_in_dim(gate_weights, source * row_count, row_count, 1)
    routed = jnp.repeat(owners == expert, TILE, axis=1, total_repeat_length=row_count)
    return jnp.where(routed, weights, jnp.zeros_like(weights))


def expert_pass(cand_rows, cand_grads, row_scale, gate_panel, up_panel):
    groups, row_total, model_width = cand_rows.shape
    quarter = gate_panel.shape[1]
    flat_rows = cand_rows.reshape(groups * row_total, model_width)
    gate_val = jnp.dot(flat_rows, gate_panel, preferred_element_type=jnp.float32)
    up_val = jnp.dot(flat_rows, up_panel, preferred_element_type=jnp.float32)
    sigmoid_val = jax.nn.sigmoid(gate_val)
    activation = gate_val * sigmoid_val
    factor = row_scale.reshape(groups * row_total, 1)
    hidden_part = (factor * activation * up_val).astype(jnp.bfloat16)
    act_grad = factor * cand_grads.reshape(groups * row_total, quarter).astype(jnp.float32)
    up_grad = (act_grad * activation).astype(jnp.bfloat16)
    gate_grad = (act_grad * up_val * sigmoid_val * (1.0 + gate_val * (1.0 - sigmoid_val))).astype(
        jnp.bfloat16
    )
    partial_value = (
        contract(gate_grad, gate_panel, 1, 1) + contract(up_grad, up_panel, 1, 1)
    ).astype(jnp.bfloat16)
    partial_value = lax.optimization_barrier(partial_value)
    grad_gate = contract(flat_rows, gate_grad, 0, 0)
    grad_up = contract(flat_rows, up_grad, 0, 0)
    return (
        partial_value.reshape(groups, row_total, model_width),
        hidden_part.reshape(groups, row_total, quarter),
        grad_gate,
        grad_up,
    )


def to_groups(tile_rows, tile_grads):
    gathered = lax.all_gather(tile_rows, DP, axis=0, tiled=True)
    quarters = core_and_chips(tile_grads, ("dp_0", "dp_1"), (1, 0), 2, 0)
    return (gathered, quarters)


def cycle_ahead(tile_rows, tile_grads):
    return shifted((tile_rows, tile_grads), "expert", 1)


def cycle_return(row_sums, hidden_part):
    return shifted((row_sums, hidden_part), "expert", -1)


def quarter_total(terms):
    return sent_and_summed(terms.astype(jnp.bfloat16), DP, 0)


def per_device(tokens, cotangent, gate_weights, tile_expert, w_gate, w_up):
    row_count = tokens.shape[1]
    cycle_size = lax.axis_size("expert")
    position = lax.axis_index("expert")
    prev_place = (position + cycle_size - 1) % cycle_size
    gate_panel = w_gate[0]
    up_panel = w_up[0]
    own_scale = route_scale(tile_expert, gate_weights, position, position, row_count)
    prev_scale = route_scale(tile_expert, gate_weights, prev_place, position, row_count)
    near_rows, near_grads = cycle_ahead(tokens, cotangent)
    cand_rows, cand_grads = to_groups(
        jnp.concatenate([tokens, near_rows], 1), jnp.concatenate([cotangent, near_grads], 1)
    )
    row_scale = jnp.concatenate([own_scale, prev_scale], 1)
    partial_value, hidden_part, grad_gate, grad_up = expert_pass(
        cand_rows, cand_grads, row_scale, gate_panel, up_panel
    )
    summed = quarter_total(partial_value.astype(jnp.float32)).astype(jnp.bfloat16)
    back_rows, back_hidden = cycle_return(summed[:, row_count:], hidden_part[:, row_count:])
    d_tokens = (summed[:, :row_count].astype(jnp.float32) + back_rows.astype(jnp.float32)).astype(
        jnp.bfloat16
    )
    hidden = (
        hidden_part[:, :row_count].astype(jnp.float32) + back_hidden.astype(jnp.float32)
    ).astype(jnp.bfloat16)
    grad_gate = (grad_gate / TILE).astype(jnp.bfloat16)[None]
    grad_up = (grad_up / TILE).astype(jnp.bfloat16)[None]
    return (d_tokens, hidden, grad_gate, grad_up)


def solution(mesh):
    split = Mesh(mesh.devices.reshape(2, 2, mesh.shape["expert"]), ("dp_0", "dp_1", "expert"))
    placed = (
        P(DP, "expert", None),
        P(DP, "expert", None),
        P(),
        P(),
        P("expert", None, DP),
        P("expert", None, DP),
    )
    return jax.shard_map(
        per_device,
        mesh=split,
        in_specs=placed,
        out_specs=(
            P(DP, "expert", None),
            P(None, "expert", DP),
            P("expert", None, DP),
            P("expert", None, DP),
        ),
        check_vma=False,
    )
```

profile of v0, /device:TPU:2, one launch (start us, length us, event | category | flops | bytes accessed | tf_op | source)
XLA Modules:
  0.0 264.4 jit_solution(17189211925136848051)
XLA Ops:
  7.2 1.7 collective-permute-start.1
  8.9 25.8 %collective-permute-done.1 = bf16[1,128,3584]{2,1,0:T(8,128)(2,1)S(1)} collective-permute-done((bf16[1,128,3584]{2,1,0:T(8,128)(2,1)}, bf16[1,128,3584]{2,1,0:T(8,128)(2,1)S(1)}, u32[]{:S(2)}, u32[]{:S(2)}) %collective-permute-start.1) | collective-permute-done | bytes 917536 | tf_op jit(solution)/shard_map/ppermute | solution.py:39
  34.7 2.5 pad_maximum_fusion
  37.8 0.8 dynamic-slice_select_fusion.1
  38.6 9.4 %collective-permute-done = bf16[1,128,1024]{1,2,0:T(8,128)(2,1)S(1)} collective-permute-done((bf16[1,128,1024]{1,2,0:T(8,128)(2,1)S(1)}, bf16[1,128,1024]{1,2,0:T(8,128)(2,1)S(1)}, u32[]{:S(2)}, u32[]{:S(2)}) %collective-permute-start) | collective-permute-done | bytes 262176 | tf_op jit(solution)/shard_map/ppermute | solution.py:39
  48.3 4.5 %all_to_all.15 = bf16[2,2,1,256,256]{4,3,0,2,1:T(8,128)(2,1)S(1)} all-to-all(bf16[2,2,1,256,256]{4,3,0,2,1:T(8,128)(2,1)S(1)} %copy.19), channel_id=1, replica_groups=mesh['dp_0'=2,'dp_1'=2,'expert'=64] {'dp_1'}, dimensions={1} | all-to-all | bytes 1048576 | tf_op jit(solution)/shard_map/all_to_all | solution.py:26
  52.7 0.8 copy.20
  53.6 4.2 %all-to-all-start.1 = ((bf16[2,2,1,256,256]{4,3,1,2,0:T(8,128)(2,1)}), bf16[2,2,1,256,256]{4,3,1,2,0:T(8,128)(2,1)S(1)}, u32[]{:S(2)}, u32[]{:S(2)}) async-start(bf16[2,2,1,256,256]{4,3,1,2,0:T(8,128)(2,1)} %copy.20), calls=%async_computation.1 | async-start | bytes 1048576 | tf_op jit(solution)/shard_map/all_to_all | solution.py:26
  57.7 44.2 %all-gather.2.cloned.1.call-done = bf16[4,256,3584]{2,1,0:T(8,128)(2,1)} async-done(((bf16[1,256,3584]{2,1,0:T(8,128)(2,1)}), bf16[4,256,3584]{2,1,0:T(8,128)(2,1)}) %all-gather.2.cloned.1.call-update) | async-done | bytes 7340048 | tf_op jit(solution)/shard_map/all_gather | solution.py:92
  101.9 6.6 %fusion.6 = f32[1024,256]{1,0:T(8,128)} fusion(bf16[1024,3584]{1,0:T(8,128)(2,1)} %bitcast.49, bf16[1,3584,256]{2,1,0:T(8,128)(2,1)} %param.20), kind=kOutput, calls=%fused_computation.10 | convolution fusion | flops 1879048192 | bytes 10223616 | tf_op jit(solution)/shard_map/dot_general | solution.py:66
  108.5 0.8 copy-done.3
  109.3 5.9 %multiply_convert_fusion = (bf16[1024,256]{1,0:T(8,128)(2,1)S(1)}, bf16[1024,256]{1,0:T(8,128)(2,1)S(1)}, bf16[1024,256]{1,0:T(8,128)(2,1)S(1)}) fusion(f32[1024]{0:T(1024)S(1)} %bitcast.48, f32[1024,256]{1,0:T(8,128)} %fusion.6, bf16[2,2,1,256,256]{4,3,1,2,0:T(8,128)(2,1)} %copy-done.3, bf16[1024,3584]{1,0:T(8,128)(2,1)} %bitcast.50, ...), kind=kOutput, calls=%fused_computation.23 | convolution fusion | flops 1883766784 | bytes 12324864 | tf_op jit(solution)/shard_map/dot_general | solution.py:67
  115.3 7.3 %fusion.4 = f32[1024,3584]{1,0:T(8,128)} fusion(bf16[1024,256]{1,0:T(8,128)(2,1)S(1)} %get-tuple-element.48, bf16[1,3584,256]{2,1,0:T(8,128)(2,1)S(1)} %copy-done.2), kind=kOutput, calls=%fused_computation.8 | convolution fusion | flops 1879048192 | bytes 17039360 | tf_op jit(solution)/shard_map/dot_general | solution.py:49
  122.6 10.2 %add_convert_fusion = bf16[1024,3584]{1,0:T(8,128)(2,1)} fusion(f32[1024,3584]{1,0:T(8,128)} %fusion.4, bf16[1024,256]{1,0:T(8,128)(2,1)S(1)} %get-tuple-element.49, bf16[1,3584,256]{2,1,0:T(8,128)(2,1)S(1)} %copy-done), kind=kOutput, calls=%fused_computation | convolution fusion | flops 1886388224 | bytes 24379392 | tf_op jit(solution)/shard_map/dot_general | solution.py:49
  132.8 5.4 %all-to-all-start.2 = ((bf16[4,1,256,3584]{3,2,1,0:T(8,128)(2,1)}), bf16[4,1,256,3584]{3,2,1,0:T(8,128)(2,1)}, u32[]{:S(2)}, u32[]{:S(2)}) async-start(bf16[4,1,256,3584]{3,2,1,0:T(8,128)(2,1)} %bitcast.42), calls=%async_computation.2 | async-start | bytes 14680064 | tf_op jit(solution)/shard_map/all_to_all | solution.py:44
  139.0 3.3 %collective-permute-start.3 = (bf16[4,128,256]{2,1,0:T(8,128)(2,1)}, bf16[4,128,256]{2,1,0:T(8,128)(2,1)}, u32[]{:S(2)}, u32[]{:S(2)}) collective-permute-start(bf16[4,128,256]{2,1,0:T(8,128)(2,1)} %slice.47), channel_id=1, source_target_pairs={{0,63},{1,0},{2,1},{3,2},{4,3},{5,4},{6,5},{7,6},{8,7},{9,8},{10,9... | collective-permute-start | bytes 786440 | tf_op jit(solution)/shard_map/ppermute | solution.py:39
  142.3 6.4 %fusion.3 = bf16[1,3584,256]{2,1,0:T(8,128)(2,1)} fusion(bf16[1024,3584]{1,0:T(8,128)(2,1)} %bitcast.51, bf16[1024,256]{1,0:T(8,128)(2,1)S(1)} %get-tuple-element.48), kind=kOutput, calls=%fused_computation.6 | convolution fusion | flops 1880883200 | bytes 9699328 | tf_op jit(solution)/shard_map/dot_general | solution.py:49
  148.8 78.5 %all-to-all-done.2 = bf16[4,1,256,3584]{3,2,1,0:T(8,128)(2,1)} async-done(((bf16[4,1,256,3584]{3,2,1,0:T(8,128)(2,1)}), bf16[4,1,256,3584]{3,2,1,0:T(8,128)(2,1)}, u32[]{:S(2)}, u32[]{:S(2)}) %all-to-all-start.2) | async-done | bytes 7340064 | tf_op jit(solution)/shard_map/all_to_all | solution.py:44
  227.3 6.0 %reduce_sum.14 = bf16[256,3584]{1,0:T(8,128)(2,1)} reduce(bf16[4,1,256,3584]{3,2,1,0:T(8,128)(2,1)} %all-to-all-done.2, bf16[]{:T(256)} %constant.151.clone.1), dimensions={0,1}, to_apply=%region_0.2 | reduce | flops 2752512 | bytes 9175042 | tf_op jit(solution)/shard_map/reduce_sum | solution.py:45
  233.3 1.2 slice.45
  234.7 6.6 %fusion.2 = bf16[1,3584,256]{2,1,0:T(8,128)(2,1)} fusion(bf16[1024,3584]{1,0:T(8,128)(2,1)} %bitcast.52, bf16[1024,256]{1,0:T(8,128)(2,1)S(1)} %get-tuple-element.49), kind=kOutput, calls=%fused_computation.5 | convolution fusion | flops 1880883200 | bytes 9699328 | tf_op jit(solution)/shard_map/dot_general | solution.py:49
  241.2 1.7 add_convert_fusion.2
  243.0 13.5 %collective-permute-done.2 = bf16[1,128,3584]{2,1,0:T(8,128)(2,1)S(1)} collective-permute-done((bf16[1,128,3584]{2,1,0:T(8,128)(2,1)S(1)}, bf16[1,128,3584]{2,1,0:T(8,128)(2,1)S(1)}, u32[]{:S(2)}, u32[]{:S(2)}) %collective-permute-start.2) | collective-permute-done | bytes 917536 | tf_op jit(solution)/shard_map/ppermute | solution.py:39
  256.5 1.1 add_convert_fusion.1
  (24 shorter events, 1.6 us)
Async XLA Ops:
  7.2 102.2 %copy-start = (bf16[1,3584,256]{2,1,0:T(8,128)(2,1)S(1)}, bf16[1,3584,256]{2,1,0:T(8,128)(2,1)}, u32[]{:S(2)}) copy-start(bf16[1,3584,256]{2,1,0:T(8,128)(2,1)} %param.21) | copy-start | bytes 5505028
  7.2 30.1 %copy-start.4 = (bf16[1,128,1024]{2,1,0:T(8,128)(2,1)S(1)}, bf16[1,128,1024]{2,1,0:T(8,128)(2,1)}, u32[]{:S(2)}) copy-start(bf16[1,128,1024]{2,1,0:T(8,128)(2,1)} %param.17) | copy-start | bytes 786436
  7.2 30.4 %copy-start.5 = (s32[4,64]{1,0:T(4,128)S(1)}, s32[4,64]{1,0:T(4,128)}, u32[]{:S(2)}) copy-start(s32[4,64]{1,0:T(4,128)} %param.19) | copy-start | bytes 3076
  7.2 94.7 %all-gather.2.cloned.1.call-start = ((), (), s32[]{:S(2)}) async-start(), calls=%async_computation.3 | async-start | bytes 9175040 | tf_op jit(solution)/shard_map/all_gather | solution.py:92
  7.2 27.5 %collective-permute-start.1 = (bf16[1,128,3584]{2,1,0:T(8,128)(2,1)}, bf16[1,128,3584]{2,1,0:T(8,128)(2,1)S(1)}, u32[]{:S(2)}, u32[]{:S(2)}) collective-permute-start(bf16[1,128,3584]{2,1,0:T(8,128)(2,1)} %param.16), channel_id=1, source_target_pairs={{0,1},{1,2},{2,3},{3,4},{4,5},{5,6},{6,7},{7,8},{8,9},{9,10},{10,1... | collective-permute-start | bytes 2752520 | tf_op jit(solution)/shard_map/ppermute | solution.py:39
  37.5 10.6 %collective-permute-start = (bf16[1,128,1024]{1,2,0:T(8,128)(2,1)S(1)}, bf16[1,128,1024]{1,2,0:T(8,128)(2,1)S(1)}, u32[]{:S(2)}, u32[]{:S(2)}) collective-permute-start(bf16[1,128,1024]{1,2,0:T(8,128)(2,1)S(1)} %copy.17), channel_id=1, source_target_pairs={{0,1},{1,2},{2,3},{3,4},{4,5},{5,6},{6,7},{7,8},{8,9},{9,10},{10,1... | collective-permute-start | bytes 786440 | tf_op jit(solution)/shard_map/ppermute | solution.py:39
  53.6 55.0 %all-to-all-start.1 = ((bf16[2,2,1,256,256]{4,3,1,2,0:T(8,128)(2,1)}), bf16[2,2,1,256,256]{4,3,1,2,0:T(8,128)(2,1)S(1)}, u32[]{:S(2)}, u32[]{:S(2)}) async-start(bf16[2,2,1,256,256]{4,3,1,2,0:T(8,128)(2,1)} %copy.20), calls=%async_computation.1 | async-start | bytes 1048576 | tf_op jit(solution)/shard_map/all_to_all | solution.py:26
  108.5 0.8 copy-start.3
  109.3 5.9 %copy-start.2 = (bf16[1,3584,256]{2,1,0:T(8,128)(2,1)S(1)}, bf16[1,3584,256]{2,1,0:T(8,128)(2,1)}, u32[]{:S(2)}) copy-start(bf16[1,3584,256]{2,1,0:T(8,128)(2,1)} %param.20) | copy-start | bytes 5505028
  132.8 94.5 %all-to-all-start.2 = ((bf16[4,1,256,3584]{3,2,1,0:T(8,128)(2,1)}), bf16[4,1,256,3584]{3,2,1,0:T(8,128)(2,1)}, u32[]{:S(2)}, u32[]{:S(2)}) async-start(bf16[4,1,256,3584]{3,2,1,0:T(8,128)(2,1)} %bitcast.42), calls=%async_computation.2 | async-start | bytes 14680064 | tf_op jit(solution)/shard_map/all_to_all | solution.py:44
  139.0 102.2 %collective-permute-start.3 = (bf16[4,128,256]{2,1,0:T(8,128)(2,1)}, bf16[4,128,256]{2,1,0:T(8,128)(2,1)}, u32[]{:S(2)}, u32[]{:S(2)}) collective-permute-start(bf16[4,128,256]{2,1,0:T(8,128)(2,1)} %slice.47), channel_id=1, source_target_pairs={{0,63},{1,0},{2,1},{3,2},{4,3},{5,4},{6,5},{7,6},{8,7},{9,8},{10,9... | collective-permute-start | bytes 786440 | tf_op jit(solution)/shard_map/ppermute | solution.py:39
  234.6 21.9 %copy-start.1 = (bf16[256,3584]{1,0:T(8,128)(2,1)S(1)}, bf16[256,3584]{1,0:T(8,128)(2,1)}, u32[]{:S(2)}) copy-start(bf16[256,3584]{1,0:T(8,128)(2,1)} %reduce_sum.14) | copy-start | bytes 5505028
  234.6 21.9 %collective-permute-start.2 = (bf16[1,128,3584]{2,1,0:T(8,128)(2,1)S(1)}, bf16[1,128,3584]{2,1,0:T(8,128)(2,1)S(1)}, u32[]{:S(2)}, u32[]{:S(2)}) collective-permute-start(bf16[1,128,3584]{2,1,0:T(8,128)(2,1)S(1)} %slice.45), channel_id=1, source_target_pairs={{0,63},{1,0},{2,1},{3,2},{4,3},{5,4},{6,5},{7,6},{8,7},{9,8},{10,9... | collective-permute-start | bytes 2752520 | tf_op jit(solution)/shard_map/ppermute | solution.py:39
Sparse Core Ops, SparseCore 0:
  37.4 64.4 all-gather.1
where the time goes:
time: 265 us; the launch traced here: 264 us
  waiting for transfers between devices  172 us (65%)
  matrix products  43.1 us (16%)
  starting transfers between devices  14.8 us (6%)
  between operations  14.2 us (5%)
  other arithmetic  12.4 us (5%)
  blocking collectives  4.45 us (2%)
  local copies, waits for them, and re-layouts  3.98 us (2%)
    all_to_all x1, waiting for transfers between devices, sent_and_summed(): pieces = lax.all_to_all(in_blocks(x, dim, count), axis, 0, 0, tiled=True)  78.5 us
    ppermute x4, waiting for transfers between devices, shifted(): return lax.ppermute(value, axis, pairs)  48.7 us
    all_gather x1, waiting for transfers between devices, to_groups(): gathered = lax.all_gather(tile_rows, DP, axis=0, tiled=True)  44.2 us
    dot_general x4, matrix products, contract(): lax.dot_general(left, right, (((left_axis,), (right_axis,)), ((), ())), p...  30.5 us
    dot_general x1, matrix products, expert_pass(): jnp.dot(flat_rows, gate_panel, preferred_element_type=jnp.float32)  6.61 us
    reduce_sum x1, other arithmetic, sent_and_summed(): return jnp.sum(pieces.astype(jnp.float32), axis=0)  6.01 us
    dot_general x1, matrix products, expert_pass(): up_val = jnp.dot(flat_rows, up_panel, preferred_element_type=jnp.float32)  5.93 us
    all_to_all x1, starting transfers between devices, sent_and_summed(): pieces = lax.all_to_all(in_blocks(x, dim, count), axis, 0, 0, tiled=True)  5.45 us
  transfers between devices with their start and end apart: 7, of which 5 were waited for; matrix products, arithmetic and copies ran while one was open for 12% of the time, Pallas kernels for 0%

commit v1 on v0

--- a/solution.py
+++ b/solution.py
@@ -89,7 +89,9 @@
 
 
 def to_groups(tile_rows, tile_grads):
-    gathered = lax.all_gather(tile_rows, DP, axis=0, tiled=True)
+    gathered = jnp.concatenate(
+        lax.all_to_all(jnp.stack([tile_rows] * lax.axis_size(DP)), DP, 0, 0), axis=0
+    )
     quarters = core_and_chips(tile_grads, ("dp_0", "dp_1"), (1, 0), 2, 0)
     return (gathered, quarters)
 

time: 265 us -> 297 us (1.12)
  waiting for transfers between devices: 172 us -> 205 us
  between operations: 14.2 us -> 0.78 us
  starting transfers between devices: 14.8 us -> 23.4 us
  local copies, waits for them, and re-layouts: 3.98 us -> 10.7 us
  blocking collectives: 4.45 us -> 0 us
    all_to_all x0 -> x1, waiting for transfers between devices: none -> 81.5 us  [to_groups(): lax.all_to_all(jnp.stack([tile_rows] * lax.axis_size(DP)), DP, 0, 0)]
    all_gather x1 -> x0, waiting for transfers between devices: 44.2 us -> none  [to_groups(): gathered = lax.all_gather(tile_rows, DP, axis=0, tiled=True)]
    ppermute x4, waiting for transfers between devices: 48.7 us -> 42.5 us  [shifted(): return lax.ppermute(value, axis, pairs)]
    all_to_all x0 -> x1, starting transfers between devices: none -> 5.59 us  [to_groups(): lax.all_to_all(jnp.stack([tile_rows] * lax.axis_size(DP)), DP, 0, 0)]
    another operation x0 -> x1, local copies, waits for them, and re-layouts: none -> 5 us  [to_groups(): jnp.stack([tile_rows] * lax.axis_size(DP))]
    all_to_all x1 -> x0, blocking collectives: 4.45 us -> none  [exchange_in_order(): out = lax.all_to_all(out, axes[k], k, k, tiled=True)]
    all_to_all x1 -> x2, starting transfers between devices: 4.16 us -> 6.98 us  [exchange_in_order(): out = lax.all_to_all(out, axes[k], k, k, tiled=True)]
  transfers between devices with their start and end apart: 7 -> 8, of which waited for: 5 -> 5; matrix products, arithmetic and copies ran while one was open for 12% -> 12% of each run, Pallas kernels for 0% -> 0%
where the time goes in v1:
time: 297 us; the launch traced here: 296 us
  waiting for transfers between devices  205 us (69%)
  matrix products  43.1 us (15%)
  starting transfers between devices  23.4 us (8%)
  other arithmetic  12.5 us (4%)
  local copies, waits for them, and re-layouts  10.7 us (4%)
    all_to_all x1, waiting for transfers between devices, to_groups(): lax.all_to_all(jnp.stack([tile_rows] * lax.axis_size(DP)), DP, 0, 0)  81.5 us
    all_to_all x1, waiting for transfers between devices, sent_and_summed(): pieces = lax.all_to_all(in_blocks(x, dim, count), axis, 0, 0, tiled=True)  78.5 us
    ppermute x4, waiting for transfers between devices, shifted(): return lax.ppermute(value, axis, pairs)  42.5 us
    dot_general x4, matrix products, contract(): lax.dot_general(left, right, (((left_axis,), (right_axis,)), ((), ())), p...  30.5 us
    all_to_all x2, starting transfers between devices, exchange_in_order(): out = lax.all_to_all(out, axes[k], k, k, tiled=True)  6.98 us
    dot_general x1, matrix products, expert_pass(): jnp.dot(flat_rows, gate_panel, preferred_element_type=jnp.float32)  6.61 us
    reduce_sum x1, other arithmetic, sent_and_summed(): return jnp.sum(pieces.astype(jnp.float32), axis=0)  6 us
  transfers between devices with their start and end apart: 8, of which 5 were waited for; matrix products, arithmetic and copies ran while one was open for 12% of the time, Pallas kernels for 0%

profile of v1, /device:TPU:2, one launch (start us, length us, event | category | flops | bytes accessed | tf_op | source)
XLA Modules:
  0.0 295.8 jit_solution(7449189479999272801)
XLA Ops:
  0.7 1.7 collective-permute-start.1
  3.4 1.9 collective-permute-start
  5.3 28.4 %collective-permute-done = bf16[1,128,1024]{1,2,0:T(8,128)(2,1)S(1)} collective-permute-done((bf16[1,128,1024]{1,2,0:T(8,128)(2,1)S(1)}, bf16[1,128,1024]{1,2,0:T(8,128)(2,1)S(1)}, u32[]{:S(2)}, u32[]{:S(2)}) %collective-permute-start) | collective-permute-done | bytes 262176 | tf_op jit(solution)/shard_map/ppermute | solution.py:39
  34.8 3.5 %all-to-all-start = ((bf16[2,2,1,256,256]{4,3,0,2,1:T(8,128)(2,1)}), bf16[2,2,1,256,256]{4,3,0,2,1:T(8,128)(2,1)S(1)}, u32[]{:S(2)}, u32[]{:S(2)}) async-start(bf16[2,2,1,256,256]{4,3,0,2,1:T(8,128)(2,1)} %copy.19), calls=%async_computation | async-start | bytes 1048576 | tf_op jit(solution)/shard_map/all_to_all | solution.py:26
  38.4 2.5 maximum_bitcast_fusion
  40.9 5.0 %stack.2 = bf16[4,1,256,3584]{3,2,1,0:T(8,128)(2,1)} broadcast(bf16[256,3584]{1,0:T(8,128)(2,1)} %maximum_bitcast_fusion), dimensions={2,3} | broadcast | bytes 9175040 | tf_op jit(solution)/shard_map/stack | solution.py:93
  45.9 5.6 %all-to-all-start.2 = ((bf16[4,1,256,3584]{3,2,1,0:T(8,128)(2,1)}), bf16[4,1,256,3584]{3,2,1,0:T(8,128)(2,1)}, u32[]{:S(2)}, u32[]{:S(2)}) async-start(bf16[4,1,256,3584]{3,2,1,0:T(8,128)(2,1)} %stack.2), calls=%async_computation.2 | async-start | bytes 14680064 | tf_op jit(solution)/shard_map/all_to_all | solution.py:93
  53.4 81.5 %all-to-all-done.2 = bf16[4,1,256,3584]{3,2,1,0:T(8,128)(2,1)} async-done(((bf16[4,1,256,3584]{3,2,1,0:T(8,128)(2,1)}), bf16[4,1,256,3584]{3,2,1,0:T(8,128)(2,1)}, u32[]{:S(2)}, u32[]{:S(2)}) %all-to-all-start.2) | async-done | bytes 7340064 | tf_op jit(solution)/shard_map/all_to_all | solution.py:93
  134.9 3.5 %all-to-all-start.1 = ((bf16[2,2,1,256,256]{4,3,1,2,0:T(8,128)(2,1)}), bf16[2,2,1,256,256]{4,3,1,2,0:T(8,128)(2,1)S(1)}, u32[]{:S(2)}, u32[]{:S(2)}) async-start(bf16[2,2,1,256,256]{4,3,1,2,0:T(8,128)(2,1)} %copy.20), calls=%async_computation.1 | async-start | bytes 1048576 | tf_op jit(solution)/shard_map/all_to_all | solution.py:26
  138.4 6.6 %fusion.6 = f32[1024,256]{1,0:T(8,128)} fusion(bf16[1024,3584]{1,0:T(8,128)(2,1)} %bitcast.5, bf16[1,3584,256]{2,1,0:T(8,128)(2,1)} %param.20), kind=kOutput, calls=%fused_computation.10 | convolution fusion | flops 1879048192 | bytes 10223616 | tf_op jit(solution)/shard_map/dot_general | solution.py:66
  145.0 2.8 all-to-all-done.1
  148.6 5.9 %multiply_convert_fusion = (bf16[1024,256]{1,0:T(8,128)(2,1)S(1)}, bf16[1024,256]{1,0:T(8,128)(2,1)S(1)}, bf16[1024,256]{1,0:T(8,128)(2,1)S(1)}) fusion(f32[1024]{0:T(1024)S(1)} %bitcast.50, f32[1024,256]{1,0:T(8,128)} %fusion.6, bf16[2,2,1,256,256]{4,3,1,2,0:T(8,128)(2,1)} %copy-done.4, bf16[1024,3584]{1,0:T(8,128)(2,1)} %bitcast.5, ...), kind=kOutput, calls=%fused_computation.23 | convolution fusion | flops 1883766784 | bytes 12324864 | tf_op jit(solution)/shard_map/dot_general | solution.py:67
  154.6 7.3 %fusion.4 = f32[1024,3584]{1,0:T(8,128)} fusion(bf16[1024,256]{1,0:T(8,128)(2,1)S(1)} %get-tuple-element.48, bf16[1,3584,256]{2,1,0:T(8,128)(2,1)S(1)} %copy-done.2), kind=kOutput, calls=%fused_computation.8 | convolution fusion | flops 1879048192 | bytes 17039360 | tf_op jit(solution)/shard_map/dot_general | solution.py:49
  161.9 10.2 %add_convert_fusion = bf16[1024,3584]{1,0:T(8,128)(2,1)} fusion(f32[1024,3584]{1,0:T(8,128)} %fusion.4, bf16[1024,256]{1,0:T(8,128)(2,1)S(1)} %get-tuple-element.49, bf16[1,3584,256]{2,1,0:T(8,128)(2,1)S(1)} %copy-done), kind=kOutput, calls=%fused_computation | convolution fusion | flops 1886388224 | bytes 24379392 | tf_op jit(solution)/shard_map/dot_general | solution.py:49
  172.1 5.4 %all-to-all-start.3 = ((bf16[4,1,256,3584]{3,2,1,0:T(8,128)(2,1)}), bf16[4,1,256,3584]{3,2,1,0:T(8,128)(2,1)}, u32[]{:S(2)}, u32[]{:S(2)}) async-start(bf16[4,1,256,3584]{3,2,1,0:T(8,128)(2,1)} %bitcast.44), calls=%async_computation.3 | async-start | bytes 14680064 | tf_op jit(solution)/shard_map/all_to_all | solution.py:44
  178.3 1.7 collective-permute-start.3
  180.0 6.4 %fusion.3 = bf16[1,3584,256]{2,1,0:T(8,128)(2,1)} fusion(bf16[1024,3584]{1,0:T(8,128)(2,1)} %bitcast.5, bf16[1024,256]{1,0:T(8,128)(2,1)S(1)} %get-tuple-element.48), kind=kOutput, calls=%fused_computation.6 | convolution fusion | flops 1880883200 | bytes 9699328 | tf_op jit(solution)/shard_map/dot_general | solution.py:49
  186.5 78.5 %all-to-all-done.3 = bf16[4,1,256,3584]{3,2,1,0:T(8,128)(2,1)} async-done(((bf16[4,1,256,3584]{3,2,1,0:T(8,128)(2,1)}), bf16[4,1,256,3584]{3,2,1,0:T(8,128)(2,1)}, u32[]{:S(2)}, u32[]{:S(2)}) %all-to-all-start.3) | async-done | bytes 7340064 | tf_op jit(solution)/shard_map/all_to_all | solution.py:44
  265.0 6.0 %reduce_sum.14 = bf16[256,3584]{1,0:T(8,128)(2,1)} reduce(bf16[4,1,256,3584]{3,2,1,0:T(8,128)(2,1)} %all-to-all-done.3, bf16[]{:T(256)} %constant.151.clone.1), dimensions={0,1}, to_apply=%region_0.2 | reduce | flops 2752512 | bytes 9175042 | tf_op jit(solution)/shard_map/reduce_sum | solution.py:45
  271.0 1.2 slice.45
  272.4 6.6 %fusion.2 = bf16[1,3584,256]{2,1,0:T(8,128)(2,1)} fusion(bf16[1024,3584]{1,0:T(8,128)(2,1)} %bitcast.5, bf16[1024,256]{1,0:T(8,128)(2,1)S(1)} %get-tuple-element.49), kind=kOutput, calls=%fused_computation.5 | convolution fusion | flops 1880883200 | bytes 9699328 | tf_op jit(solution)/shard_map/dot_general | solution.py:49
  278.9 1.7 add_convert_fusion.2
  280.7 14.0 %collective-permute-done.2 = bf16[1,128,3584]{2,1,0:T(8,128)(2,1)S(1)} collective-permute-done((bf16[1,128,3584]{2,1,0:T(8,128)(2,1)S(1)}, bf16[1,128,3584]{2,1,0:T(8,128)(2,1)S(1)}, u32[]{:S(2)}, u32[]{:S(2)}) %collective-permute-start.2) | collective-permute-done | bytes 917536 | tf_op jit(solution)/shard_map/ppermute | solution.py:39
  294.7 1.1 add_convert_fusion.1
  (25 shorter events, 5.7 us)
Async XLA Ops:
  0.6 148.0 %copy-start = (bf16[1,3584,256]{2,1,0:T(8,128)(2,1)S(1)}, bf16[1,3584,256]{2,1,0:T(8,128)(2,1)}, u32[]{:S(2)}) copy-start(bf16[1,3584,256]{2,1,0:T(8,128)(2,1)} %param.21) | copy-start | bytes 5505028
  0.6 37.7 %copy-start.3 = (bf16[1,128,3584]{2,1,0:T(8,128)(2,1)S(1)}, bf16[1,128,3584]{2,1,0:T(8,128)(2,1)}, u32[]{:S(2)}) copy-start(bf16[1,128,3584]{2,1,0:T(8,128)(2,1)} %param.16) | copy-start | bytes 2752516
  0.7 37.7 %collective-permute-start.1 = (bf16[1,128,3584]{2,1,0:T(8,128)(2,1)}, bf16[1,128,3584]{2,1,0:T(8,128)(2,1)}, u32[]{:S(2)}, u32[]{:S(2)}) collective-permute-start(bf16[1,128,3584]{2,1,0:T(8,128)(2,1)} %param.16), channel_id=1, source_target_pairs={{0,1},{1,2},{2,3},{3,4},{4,5},{5,6},{6,7},{7,8},{8,9},{9,10},{10,1... | collective-permute-start | bytes 2752520 | tf_op jit(solution)/shard_map/ppermute | solution.py:39
  3.4 30.3 %collective-permute-start = (bf16[1,128,1024]{1,2,0:T(8,128)(2,1)S(1)}, bf16[1,128,1024]{1,2,0:T(8,128)(2,1)S(1)}, u32[]{:S(2)}, u32[]{:S(2)}) collective-permute-start(bf16[1,128,1024]{1,2,0:T(8,128)(2,1)S(1)} %copy.17), channel_id=1, source_target_pairs={{0,1},{1,2},{2,3},{3,4},{4,5},{5,6},{6,7},{7,8},{8,9},{9,10},{10,1... | collective-permute-start | bytes 786440 | tf_op jit(solution)/shard_map/ppermute | solution.py:39
  34.8 6.0 %all-to-all-start = ((bf16[2,2,1,256,256]{4,3,0,2,1:T(8,128)(2,1)}), bf16[2,2,1,256,256]{4,3,0,2,1:T(8,128)(2,1)S(1)}, u32[]{:S(2)}, u32[]{:S(2)}) async-start(bf16[2,2,1,256,256]{4,3,0,2,1:T(8,128)(2,1)} %copy.19), calls=%async_computation | async-start | bytes 1048576 | tf_op jit(solution)/shard_map/all_to_all | solution.py:26
  45.9 5.6 %copy-start.5 = (s32[4,64]{1,0:T(4,128)S(1)}, s32[4,64]{1,0:T(4,128)}, u32[]{:S(2)}) copy-start(s32[4,64]{1,0:T(4,128)} %param.19) | copy-start | bytes 3076
  45.9 89.0 %all-to-all-start.2 = ((bf16[4,1,256,3584]{3,2,1,0:T(8,128)(2,1)}), bf16[4,1,256,3584]{3,2,1,0:T(8,128)(2,1)}, u32[]{:S(2)}, u32[]{:S(2)}) async-start(bf16[4,1,256,3584]{3,2,1,0:T(8,128)(2,1)} %stack.2), calls=%async_computation.2 | async-start | bytes 14680064 | tf_op jit(solution)/shard_map/all_to_all | solution.py:93
  134.9 12.9 %all-to-all-start.1 = ((bf16[2,2,1,256,256]{4,3,1,2,0:T(8,128)(2,1)}), bf16[2,2,1,256,256]{4,3,1,2,0:T(8,128)(2,1)S(1)}, u32[]{:S(2)}, u32[]{:S(2)}) async-start(bf16[2,2,1,256,256]{4,3,1,2,0:T(8,128)(2,1)} %copy.20), calls=%async_computation.1 | async-start | bytes 1048576 | tf_op jit(solution)/shard_map/all_to_all | solution.py:26
  147.8 0.8 copy-start.4
  148.6 5.9 %copy-start.2 = (bf16[1,3584,256]{2,1,0:T(8,128)(2,1)S(1)}, bf16[1,3584,256]{2,1,0:T(8,128)(2,1)}, u32[]{:S(2)}) copy-start(bf16[1,3584,256]{2,1,0:T(8,128)(2,1)} %param.20) | copy-start | bytes 5505028
  172.1 92.9 %all-to-all-start.3 = ((bf16[4,1,256,3584]{3,2,1,0:T(8,128)(2,1)}), bf16[4,1,256,3584]{3,2,1,0:T(8,128)(2,1)}, u32[]{:S(2)}, u32[]{:S(2)}) async-start(bf16[4,1,256,3584]{3,2,1,0:T(8,128)(2,1)} %bitcast.44), calls=%async_computation.3 | async-start | bytes 14680064 | tf_op jit(solution)/shard_map/all_to_all | solution.py:44
  178.3 100.6 %collective-permute-start.3 = (bf16[4,128,256]{2,1,0:T(8,128)(2,1)}, bf16[4,128,256]{2,1,0:T(8,128)(2,1)}, u32[]{:S(2)}, u32[]{:S(2)}) collective-permute-start(bf16[4,128,256]{2,1,0:T(8,128)(2,1)} %slice.47), channel_id=1, source_target_pairs={{0,63},{1,0},{2,1},{3,2},{4,3},{5,4},{6,5},{7,6},{8,7},{9,8},{10,9... | collective-permute-start | bytes 786440 | tf_op jit(solution)/shard_map/ppermute | solution.py:39
  272.3 22.4 %copy-start.1 = (bf16[256,3584]{1,0:T(8,128)(2,1)S(1)}, bf16[256,3584]{1,0:T(8,128)(2,1)}, u32[]{:S(2)}) copy-start(bf16[256,3584]{1,0:T(8,128)(2,1)} %reduce_sum.14) | copy-start | bytes 5505028
  272.3 22.4 %collective-permute-start.2 = (bf16[1,128,3584]{2,1,0:T(8,128)(2,1)S(1)}, bf16[1,128,3584]{2,1,0:T(8,128)(2,1)S(1)}, u32[]{:S(2)}, u32[]{:S(2)}) collective-permute-start(bf16[1,128,3584]{2,1,0:T(8,128)(2,1)S(1)} %slice.45), channel_id=1, source_target_pairs={{0,63},{1,0},{2,1},{3,2},{4,3},{5,4},{6,5},{7,6},{8,7},{9,8},{10,9... | collective-permute-start | bytes 2752520 | tf_op jit(solution)/shard_map/ppermute | solution.py:39
